TPU v7x, 128 devices: a whole 4x4x4 slice. The times are simulated.
128 devices in a mesh: row: 8 (over x, core), col: 16 (over y, z).
Axes of the slice: x: 4, y: 4, z: 4, core: 2. Of those that a mesh axis runs over, the one named last changes fastest.
Arguments:
- front_blocks: float32 [16, 1024, 8, 2048], P(None, 'row', None, 'col'), may hold values from -2.5 to 10.5, as said below
- child_updates: bfloat16 [2, 12, 1024, 6, 2048], P(None, None, 'row', None, 'col'), may hold values from -0.2 to 2.2, as said below
- child_map: int32 [2, 96], replicated, may hold values from 0 to 127, as said below
Outputs:
- factored: float32 [16, 1024, 8, 2048], P(None, 'row', None, 'col')
Inputs may be any that keep to these rules, and one draw needn't show every extreme that they name: `child_map`: for each child, block a * 16 + j (0 <= j < 16) lands in front block h_a * 16 + ((s_a - j) mod 16), with 6 distinct h_a below 8 and s_a = (s + q_a) mod 16, q a permutation of 0 .. 5. Hence along col one device sends at most 1 of a child's column blocks to one device, along row at most 2 of its row blocks, and both bounds are reached in every draw. `front_blocks`: symmetric positive definite. `child_updates`: each child update is symmetric.
All inputs are finite; a program needn't handle non-finite values.
Results may differ from a plain program's by a relative error of at most 0.0003.
Values may be sent and summed in bfloat16 or wider, within the bound.
A program may use at most 192 MiB of HBM per device.

v0:
```python
import jax
import jax.numpy as jnp
from jax import lax
from jax.sharding import PartitionSpec as P

PW = 256
PANELS = 2
PD = 512


def spread_2(value, axis, source):
    kept = jnp.where(lax.axis_index(axis) == source, value, 0).astype(value.dtype)
    return lax.psum(kept, axis)


def earlier_count(targets):
    count_all = targets.shape[1]
    matches = targets[:, :, None, :] == targets[:, None, :, :]
    order_ids = jnp.arange(count_all)
    before = (order_ids[None, :] < order_ids[:, None])[None, :, :, None]
    return jnp.sum(matches & before, axis=2)


def arrival_info(block_map, my_index, devices):
    child_count = block_map.shape[0]
    slot_total = block_map.shape[1] // devices
    block_grid = block_map.reshape(child_count, slot_total, devices)
    targets = block_grid % devices
    home_slots = block_grid // devices
    arriving = targets == my_index
    arrival_flat = arriving.reshape(child_count, slot_total * devices).astype(jnp.int32)
    positions = (jnp.cumsum(arrival_flat, axis=1) - 1).reshape(child_count, slot_total, devices)
    return (targets, home_slots, arriving, positions)


def route_tables(block_map, my_index, devices, capacity, slot_count):
    child_count = block_map.shape[0]
    slot_total = block_map.shape[1] // devices
    targets, home_slots, arriving, positions = arrival_info(block_map, my_index, devices)
    slot_ranks = earlier_count(targets)
    my_targets = lax.dynamic_index_in_dim(targets, my_index, axis=2, keepdims=False)
    my_ranks = lax.dynamic_index_in_dim(slot_ranks, my_index, axis=2, keepdims=False)
    child_ids = jnp.arange(child_count)[:, None]
    slot_values = jnp.broadcast_to(
        jnp.arange(slot_total, dtype=jnp.int32)[None, :], (child_count, slot_total)
    )
    send_index = jnp.full((child_count, devices * capacity), slot_total, jnp.int32)
    send_index = send_index.at[child_ids, my_targets * capacity + my_ranks].set(slot_values)
    sources = jnp.arange(devices, dtype=jnp.int32)[None, None, :]
    where_from = jnp.where(arriving, sources * capacity + slot_ranks, devices * capacity)
    where_to = jnp.where(arriving, home_slots, slot_count)
    place_index = jnp.full((child_count, slot_count + 1), devices * capacity, jnp.int32)
    place_index = place_index.at[child_ids[:, :, None], where_to].set(where_from)
    return (send_index, place_index[:, :slot_count])


def pick_slots(payload, index_table, axis_no):
    return jax.vmap(lambda part_data, part_index: jnp.take(part_data, part_index, axis=axis_no))(
        payload, index_table
    )


def move_rows(payload, block_map, slot_count):
    devices = lax.axis_size("row")
    my_index = lax.axis_index("row")
    col_devices = lax.axis_size("col")
    child_count, slot_total, tile_size, row_width = payload.shape
    col_slots = block_map.shape[1] // col_devices
    capacity = col_devices // devices * ((col_slots + devices - 1) // devices)
    send_index, place_index = route_tables(block_map, my_index, devices, capacity, slot_count)
    padded = jnp.concatenate(
        [payload, jnp.zeros((child_count, 1, tile_size, row_width), payload.dtype)], axis=1
    )
    outgoing = pick_slots(padded, send_index, 0).reshape(
        child_count, devices * capacity * tile_size, row_width
    )
    incoming = lax.all_to_all(outgoing, "row", split_axis=1, concat_axis=1, tiled=True)
    incoming = incoming.reshape(child_count, devices * capacity, tile_size, row_width)
    padded_in = jnp.concatenate(
        [incoming, jnp.zeros((child_count, 1, tile_size, row_width), incoming.dtype)], axis=1
    )
    return pick_slots(padded_in, place_index, 0)


def move_columns(payload, block_map, slot_count):
    devices = lax.axis_size("col")
    my_index = lax.axis_index("col")
    child_count, height, slot_total, tile_size = payload.shape
    capacity = (slot_total + devices - 1) // devices
    send_index, place_index = route_tables(block_map, my_index, devices, capacity, slot_count)
    padded = jnp.concatenate(
        [payload, jnp.zeros((child_count, height, 1, tile_size), payload.dtype)], axis=2
    )
    outgoing = pick_slots(padded, send_index, 1).reshape(
        child_count, height, devices * capacity * tile_size
    )
    incoming = lax.all_to_all(outgoing, "col", split_axis=2, concat_axis=2, tiled=True)
    incoming = incoming.reshape(child_count, height, devices * capacity, tile_size)
    padded_in = jnp.concatenate(
        [incoming, jnp.zeros((child_count, height, 1, tile_size), incoming.dtype)], axis=2
    )
    return pick_slots(padded_in, place_index, 1)


def on_device(front_blocks, child_updates, child_map):
    row_count = lax.axis_size("row")
    col_count = lax.axis_size("col")
    row_index = lax.axis_index("row")
    col_index = lax.axis_index("col")
    front_slots_r = front_blocks.shape[0]
    tile_size = front_blocks.shape[1]
    front_slots_c = front_blocks.shape[2]
    child_count = child_updates.shape[0]
    child_rows = child_updates.shape[1]
    child_cols = child_updates.shape[3]
    arrived = move_rows(
        child_updates.reshape(child_count, child_rows, tile_size, child_cols * tile_size),
        child_map,
        front_slots_r,
    )
    arrived = move_columns(
        arrived.reshape(child_count, front_slots_r * tile_size, child_cols, tile_size),
        child_map,
        front_slots_c,
    )
    height = front_slots_r * tile_size
    breadth = front_slots_c * tile_size
    children_sum = jnp.sum(arrived.astype(jnp.float32), axis=0).reshape(height, breadth)
    assembled = front_blocks.reshape(height, breadth) + children_sum
    local_rows = jnp.arange(height, dtype=jnp.int32)
    row_global = (
        local_rows // tile_size * row_count + row_index
    ) * tile_size + local_rows % tile_size
    local_cols = jnp.arange(breadth, dtype=jnp.int32)
    col_global = (
        local_cols // tile_size * col_count + col_index
    ) * tile_size + local_cols % tile_size
    panel_tiles = PW // tile_size
    spread = col_count // row_count
    row_factors = []
    col_factors = []
    for panel_no in range(PANELS):
        first_col = panel_no * PW
        finish = first_col + PW
        column_tiles = []
        for tile_no in range(panel_tiles):
            global_tile = panel_no * panel_tiles + tile_no
            col_slot = global_tile // col_count
            column_tile = assembled[:, col_slot * tile_size : (col_slot + 1) * tile_size]
            column_tiles.append(column_tile)
        pieces = [
            jnp.where(
                col_index == (panel_no * panel_tiles + tile_no) % col_count,
                column_tiles[tile_no],
                0.0,
            )
            for tile_no in range(panel_tiles)
        ]
        panel_rows = lax.psum(jnp.concatenate(pieces, axis=1), "col")
        diag_pieces = []
        for tile_no in range(panel_tiles):
            global_tile = panel_no * panel_tiles + tile_no
            row_slot = global_tile // row_count
            diag_pieces.append(
                jnp.where(
                    row_index == global_tile % row_count,
                    panel_rows[row_slot * tile_size : (row_slot + 1) * tile_size],
                    0.0,
                )
            )
        diagonal = lax.psum(jnp.concatenate(diag_pieces, axis=0), "row")
        factor = jnp.linalg.cholesky(diagonal)
        solved = lax.linalg.triangular_solve(
            factor, panel_rows, left_side=False, lower=True, transpose_a=True
        )
        lower_part = jnp.where(row_global[:, None] >= finish, solved, 0.0)
        inside = (row_global >= first_col) & (row_global < finish)
        factor_rows = jnp.take(factor, jnp.clip(row_global - first_col, 0, PW - 1), axis=0)
        lower_part = jnp.where(inside[:, None], factor_rows, lower_part)
        chosen = lax.dynamic_index_in_dim(
            lower_part.reshape(front_slots_c, spread, tile_size, PW),
            col_index // row_count,
            axis=1,
            keepdims=False,
        ).reshape(breadth, PW)
        col_part = spread_2(chosen, "row", col_index % row_count)
        assembled = assembled - jnp.dot(
            lower_part,
            col_part.T,
            precision=lax.Precision.HIGHEST,
            preferred_element_type=jnp.float32,
        )
        row_factors.append(lower_part)
        col_factors.append(col_part)
    result = assembled
    for panel_no in range(PANELS):
        for tile_no in range(panel_tiles):
            global_tile = panel_no * panel_tiles + tile_no
            col_slot = global_tile // col_count
            owner_here = col_index == global_tile % col_count
            current = result[:, col_slot * tile_size : (col_slot + 1) * tile_size]
            fresh = row_factors[panel_no][:, tile_no * tile_size : (tile_no + 1) * tile_size]
            result = result.at[:, col_slot * tile_size : (col_slot + 1) * tile_size].set(
                jnp.where(owner_here, fresh, current)
            )
    upper_mask = (row_global[:, None] < PD) & (col_global[None, :] >= PD)
    result = jnp.where(upper_mask, 0.0, result)
    return result.reshape(front_slots_r, tile_size, front_slots_c, tile_size)


def solution(mesh):
    placed = (P(None, "row", None, "col"), P(None, None, "row", None, "col"), P())
    return jax.shard_map(
        on_device,
        mesh=mesh,
        in_specs=placed,
        out_specs=P(None, "row", None, "col"),
        check_vma=False,
    )
```

profile of v0, /device:TPU:0, one launch (start us, length us, event | category | flops | bytes accessed | tf_op | source)
XLA Modules:
  0.0 1366.0 jit_solution(4621265916315295728)
XLA Ops:
  13.6 6.6 copy.72
  20.2 5.1 concatenate.51
  25.4 6.5 gather_fusion
  31.9 8.7 copy.73
  40.8 9.3 scatter_fusion.2
  54.3 44.7 %copy.74 = bf16[2,2048,768]{2,0,1:T(2,128)(2,1)} copy(bf16[2,2048,768]{2,1,0:T(8,128)(2,1)S(1)} %bitcast_select_fusion.1) | data formatting | bytes 12582912 | tf_op jit(solution)/shard_map/vmap(jit(_take))/select_n | solution.py:58
  99.0 4.9 all-to-all-start
  104.3 71.8 %all-to-all-done = bf16[2,2048,768]{2,0,1:T(2,128)(2,1)} async-done(((bf16[2,2048,768]{2,0,1:T(2,128)(2,1)}), bf16[2,2048,768]{2,0,1:T(2,128)(2,1)}, u32[]{:S(2)}, u32[]{:S(2)}) %all-to-all-start) | async-done | bytes 6291488 | tf_op jit(solution)/shard_map/all_to_all | solution.py:77
  183.5 6.5 gather_fusion.1
  190.0 13.6 reshape.731
  203.6 5.3 copy_select_fusion
  212.6 10.3 gather_fusion.2
  222.9 22.5 %copy.78 = bf16[2,2048,16,128]{1,3,2,0:T(8,128)(2,1)} copy(bf16[2,2048,16,128]{3,1,2,0:T(8,128)(2,1)} %bitcast.147) | data formatting | bytes 33554432 | tf_op jit(solution)/shard_map/vmap(jit(_take))/gather | solution.py:58
  245.4 8.5 bitcast_select_fusion
  253.9 48.9 %copy.79 = bf16[2,2048,2048]{1,0,2:T(2,128)(2,1)} copy(bf16[2,2048,2048]{1,2,0:T(8,128)(2,1)S(1)} %bitcast_select_fusion) | data formatting | bytes 33554432 | tf_op jit(solution)/shard_map/vmap(jit(_take))/select_n | solution.py:58
  302.8 8.3 all-to-all-start.1
  311.7 9.3 scatter_fusion
  321.1 8.9 copy.116
  330.0 9.2 copy.94
  339.1 263.8 %all-to-all-done.1 = bf16[2,2048,2048]{1,0,2:T(2,128)(2,1)} async-done(((bf16[2,2048,2048]{1,0,2:T(2,128)(2,1)}), bf16[2,2048,2048]{1,0,2:T(2,128)(2,1)}, u32[]{:S(2)}, u32[]{:S(2)}) %all-to-all-start.1) | async-done | bytes 16777248 | tf_op jit(solution)/shard_map/all_to_all | solution.py:97
  602.9 41.1 %copy.81 = bf16[2,2048,16,128]{3,1,2,0:T(8,128)(2,1)} copy(bf16[2,2048,16,128]{1,0,3,2:T(2,128)(2,1)} %bitcast.9) | data formatting | bytes 33554432 | tf_op jit(solution)/shard_map/reshape | solution.py:98
  644.0 15.5 %concatenate.54 = bf16[2,2048,17,128]{3,1,2,0:T(8,128)(2,1)} pad(bf16[2,2048,16,128]{3,1,2,0:T(8,128)(2,1)} %copy.81, bf16[]{:T(256)} %constant.419.clone.1), padding=0_0x0_0x0_1x0_0 | pad | bytes 34603008 | tf_op jit(solution)/shard_map/concatenate | solution.py:99
  659.5 11.1 gather_fusion.3
  670.6 9.8 convert_reduce_fusion
  680.4 9.1 copy.82
  689.5 11.7 bitcast_add_fusion
  704.3 94.6 %all-reduce.12.cloned.1.call-done = f32[2048,256]{0,1:T(8,128)} async-done(((f32[2048,256]{0,1:T(8,128)}), f32[2048,256]{0,1:T(8,128)}) %all-reduce.12.cloned.1.call-update) | async-done | bytes 2097168 | tf_op jit(solution)/shard_map/psum | solution.py:159
  801.1 59.3 %all-reduce.14.cloned.1.call-done = f32[256,256]{0,1:T(8,128)} async-done(((f32[256,256]{0,1:T(8,128)}), f32[256,256]{0,1:T(8,128)}) %all-reduce.14.cloned.1.call-update) | async-done | bytes 262160 | tf_op jit(solution)/shard_map/psum | solution.py:171
  862.5 11.7 cholesky.130
  874.2 9.8 custom-call.29
  884.5 11.7 cholesky.147
  898.9 6.8 gather_fusion.4
  911.5 19.7 %custom-call.30 = f32[2,128,128]{1,2,0:T(8,128)S(1)} custom-call(f32[2,128,128]{2,1,0:T(8,128)S(1)} %get-tuple-element.70), custom_call_target="InvertDiagBlocksLowerTriangular" | custom-call | tf_op jit(solution)/shard_map/triangular_solve/custom-call.0 | solution.py:173
  940.1 4.8 fusion.3
  946.2 61.6 %all-reduce.16.cloned.1.call-done = f32[1024,256]{0,1:T(8,128)} async-done(((f32[1024,256]{0,1:T(8,128)}), f32[1024,256]{0,1:T(8,128)}) %all-reduce.16.cloned.1.call-update) | async-done | bytes 1048592 | tf_op jit(solution)/shard_map/psum | solution.py:13
  1007.7 10.8 convolution_subtract_fusion.1
  1023.7 89.8 %all-reduce.18.cloned.1.call-done = f32[2048,256]{0,1:T(8,128)} async-done(((f32[2048,256]{0,1:T(8,128)}), f32[2048,256]{0,1:T(8,128)}) %all-reduce.18.cloned.1.call-update) | async-done | bytes 2097168 | tf_op jit(solution)/shard_map/psum | solution.py:159
  1115.3 59.6 %all-reduce.20.cloned.1.call-done = f32[256,256]{0,1:T(8,128)} async-done(((f32[256,256]{0,1:T(8,128)}), f32[256,256]{0,1:T(8,128)}) %all-reduce.20.cloned.1.call-update) | async-done | bytes 262160 | tf_op jit(solution)/shard_map/psum | solution.py:171
  1176.9 11.7 cholesky.164
  1188.7 9.8 custom-call.31
  1199.0 11.7 cholesky.181
  1213.3 8.8 gather_fusion.5
  1228.9 19.7 %custom-call.32 = f32[2,128,128]{1,2,0:T(8,128)S(1)} custom-call(f32[2,128,128]{2,1,0:T(8,128)S(1)} %get-tuple-element.71), custom_call_target="InvertDiagBlocksLowerTriangular" | custom-call | tf_op jit(solution)/shard_map/triangular_solve/custom-call.0 | solution.py:173
  1260.1 4.8 fusion.4
  1266.8 60.9 %all-reduce.22.cloned.1.call-done = f32[1024,256]{0,1:T(8,128)} async-done(((f32[1024,256]{0,1:T(8,128)}), f32[1024,256]{0,1:T(8,128)}) %all-reduce.22.cloned.1.call-update) | async-done | bytes 1048592 | tf_op jit(solution)/shard_map/psum | solution.py:13
  1327.7 10.8 convolution_subtract_fusion
  1343.0 5.2 copy.105
  1348.2 10.7 copy.90
  (153 shorter events, 91.7 us)
Async XLA Ops:
  99.0 77.1 %all-to-all-start = ((bf16[2,2048,768]{2,0,1:T(2,128)(2,1)}), bf16[2,2048,768]{2,0,1:T(2,128)(2,1)}, u32[]{:S(2)}, u32[]{:S(2)}) async-start(bf16[2,2048,768]{2,0,1:T(2,128)(2,1)} %copy.74), calls=%async_computation | async-start | bytes 12582912 | tf_op jit(solution)/shard_map/all_to_all | solution.py:77
  302.8 8.6 copy-start.4
  302.8 300.2 %all-to-all-start.1 = ((bf16[2,2048,2048]{1,0,2:T(2,128)(2,1)}), bf16[2,2048,2048]{1,0,2:T(2,128)(2,1)}, u32[]{:S(2)}, u32[]{:S(2)}) async-start(bf16[2,2048,2048]{1,0,2:T(2,128)(2,1)} %copy.79), calls=%async_computation.1 | async-start | bytes 33554432 | tf_op jit(solution)/shard_map/all_to_all | solution.py:97
  311.1 487.8 %all-reduce.12.cloned.1.call-start = ((), (), s32[]{:S(2)}) async-start(), calls=%async_computation.2 | async-start | bytes 4194304 | tf_op jit(solution)/shard_map/psum | solution.py:159
  704.2 156.2 %all-reduce.14.cloned.1.call-start = ((), (), s32[]{:S(2)}) async-start(), calls=%async_computation.3 | async-start | bytes 524288 | tf_op jit(solution)/shard_map/psum | solution.py:171
  800.6 207.2 %all-reduce.16.cloned.1.call-start = ((), (), s32[]{:S(2)}) async-start(), calls=%async_computation.4 | async-start | bytes 2097152 | tf_op jit(solution)/shard_map/psum | solution.py:13
  931.2 5.8 copy-start.3
  946.1 167.4 %all-reduce.18.cloned.1.call-start = ((), (), s32[]{:S(2)}) async-start(), calls=%async_computation.5 | async-start | bytes 4194304 | tf_op jit(solution)/shard_map/psum | solution.py:159
  1018.5 3.4 copy-start
  1023.7 151.2 %all-reduce.20.cloned.1.call-start = ((), (), s32[]{:S(2)}) async-start(), calls=%async_computation.6 | async-start | bytes 524288 | tf_op jit(solution)/shard_map/psum | solution.py:171
  1115.2 212.5 %all-reduce.22.cloned.1.call-start = ((), (), s32[]{:S(2)}) async-start(), calls=%async_computation.7 | async-start | bytes 2097152 | tf_op jit(solution)/shard_map/psum | solution.py:13
  1248.6 5.8 copy-start.2
  1338.5 2.0 copy-start.1
Sparse Core Ops, SparseCore 0:
  704.3 94.5 all-reduce.11
  801.3 58.9 all-reduce.13
  946.2 61.4 all-reduce.15
  1023.8 89.7 all-reduce.17
  1115.8 58.9 all-reduce.19
  1266.2 61.4 all-reduce.21
where the time goes:
time: 1380 us; the launch traced here: 1370 us
  waiting for transfers between devices  761 us (55%)
  local copies, waits for them, and re-layouts  364 us (26%)
  other arithmetic  176 us (13%)
  matrix products  34.1 us (2%)
  between operations  16.9 us (1%)
  starting transfers between devices  14.1 us (1%)
    all_to_all x1, waiting for transfers between devices, move_columns(): lax.all_to_all(outgoing, 'col', split_axis=2, concat_axis=2, tiled=True)  264 us
    psum x2, waiting for transfers between devices, on_device(): panel_rows = lax.psum(jnp.concatenate(pieces, axis=1), 'col')  184 us
    psum x2, waiting for transfers between devices, spread_2(): return lax.psum(kept, axis)  122 us
    psum x2, waiting for transfers between devices, on_device(): diagonal = lax.psum(jnp.concatenate(diag_pieces, axis=0), 'row')  119 us
    select_n x2, local copies, waits for them, and re-layouts, pick_slots(): jnp.take(part_data, part_index, axis=axis_no)  93.5 us
    gather x11, local copies, waits for them, and re-layouts, pick_slots(): jnp.take(part_data, part_index, axis=axis_no)  79.5 us
    all_to_all x1, waiting for transfers between devices, move_rows(): lax.all_to_all(outgoing, 'row', split_axis=1, concat_axis=1, tiled=True)  71.8 us
    another operation x14, other arithmetic, on_device(): factor = jnp.linalg.cholesky(diagonal)  69.2 us
  transfers between devices with their start and end apart: 8, of which 8 were waited for; matrix products, arithmetic and copies ran while one was open for 2% of the time, Pallas kernels for 0%

commit v1 on v0

--- a/solution.py
+++ b/solution.py
@@ -94,7 +94,9 @@
     outgoing = pick_slots(padded, send_index, 1).reshape(
         child_count, height, devices * capacity * tile_size
     )
-    incoming = lax.all_to_all(outgoing, "col", split_axis=2, concat_axis=2, tiled=True)
+    incoming = jnp.concatenate(
+        lax.all_to_all(jnp.stack(jnp.split(outgoing, lax.axis_size("col"), 2), 0), "col", 0, 0), 2
+    )
     incoming = incoming.reshape(child_count, height, devices * capacity, tile_size)
     padded_in = jnp.concatenate(
         [incoming, jnp.zeros((child_count, height, 1, tile_size), incoming.dtype)], axis=2

time: 1380 us -> 1290 us (0.935)
  local copies, waits for them, and re-layouts: 364 us -> 281 us
    select_n x2 -> x1, local copies, waits for them, and re-layouts: 93.5 us -> 44.7 us  [pick_slots(): jnp.take(part_data, part_index, axis=axis_no)]
    reshape x1 -> x0, local copies, waits for them, and re-layouts: 41.1 us -> none  [move_columns(): incoming.reshape(child_count, height, devices * capacity, tile_size)]
    unnamed x21 -> x36, local copies, waits for them, and re-layouts: 26.7 us -> 42.8 us
where the time goes in v1:
time: 1290 us; the launch traced here: 1280 us
  waiting for transfers between devices  761 us (59%)
  local copies, waits for them, and re-layouts  281 us (22%)
  other arithmetic  176 us (14%)
  matrix products  34.2 us (3%)
  between operations  16.8 us (1%)
  starting transfers between devices  14.1 us (1%)
    all_to_all x1, waiting for transfers between devices, move_columns(): lax.all_to_all(jnp.stack(jnp.split(outgoing, lax.axis_size('col'), 2), 0)...  264 us
    psum x2, waiting for transfers between devices, on_device(): panel_rows = lax.psum(jnp.concatenate(pieces, axis=1), 'col')  184 us
    psum x2, waiting for transfers between devices, spread_2(): return lax.psum(kept, axis)  122 us
    psum x2, waiting for transfers between devices, on_device(): diagonal = lax.psum(jnp.concatenate(diag_pieces, axis=0), 'row')  119 us
    gather x11, local copies, waits for them, and re-layouts, pick_slots(): jnp.take(part_data, part_index, axis=axis_no)  79.5 us
    all_to_all x1, waiting for transfers between devices, move_rows(): lax.all_to_all(outgoing, 'row', split_axis=1, concat_axis=1, tiled=True)  71.8 us
    another operation x14, other arithmetic, on_device(): factor = jnp.linalg.cholesky(diagonal)  69.2 us
    select_n x1, local copies, waits for them, and re-layouts, pick_slots(): jnp.take(part_data, part_index, axis=axis_no)  44.7 us
  transfers between devices with their start and end apart: 8, of which 8 were waited for; matrix products, arithmetic and copies ran while one was open for 2% of the time, Pallas kernels for 0%

profile of v1, /device:TPU:0, one launch (start us, length us, event | category | flops | bytes accessed | tf_op | source)
XLA Modules:
  0.0 1283.4 jit_solution(4071171554578456056)
XLA Ops:
  13.6 6.6 copy.67
  20.2 5.1 concatenate.51
  25.4 6.5 gather_fusion
  31.9 8.7 copy.68
  40.8 9.3 scatter_fusion.2
  50.2 4.1 bitcast_select_fusion.1
  54.3 44.7 %copy.69 = bf16[2,2048,768]{2,0,1:T(2,128)(2,1)} copy(bf16[2,2048,768]{2,1,0:T(8,128)(2,1)S(1)} %bitcast_select_fusion.1) | data formatting | bytes 12582912 | tf_op jit(solution)/shard_map/vmap(jit(_take))/select_n | solution.py:58
  99.0 4.9 all-to-all-start
  104.3 71.8 %all-to-all-done = bf16[2,2048,768]{2,0,1:T(2,128)(2,1)} async-done(((bf16[2,2048,768]{2,0,1:T(2,128)(2,1)}), bf16[2,2048,768]{2,0,1:T(2,128)(2,1)}, u32[]{:S(2)}, u32[]{:S(2)}) %all-to-all-start) | async-done | bytes 6291488 | tf_op jit(solution)/shard_map/all_to_all | solution.py:77
  183.5 6.5 gather_fusion.1
  190.0 13.6 %reshape.731 = bf16[2,2048,6,128]{3,2,1,0:T(8,128)(2,1)} reshape(bf16[32,128,768]{2,1,0:T(8,128)(2,1)} %gather_fusion.1) | data formatting | bytes 12582912 | tf_op jit(solution)/shard_map/vmap(jit(_take))/gather | solution.py:58
  203.6 5.3 copy_select_fusion
  212.6 10.3 gather_fusion.2
  222.9 22.5 %copy.73 = bf16[2,2048,16,128]{1,3,2,0:T(8,128)(2,1)} copy(bf16[2,2048,16,128]{3,1,2,0:T(8,128)(2,1)} %bitcast.212) | data formatting | bytes 33554432 | tf_op jit(solution)/shard_map/vmap(jit(_take))/gather | solution.py:58
  245.4 8.5 bitcast_select_fusion
  271.0 8.3 all-to-all-start.1
  279.9 9.3 scatter_fusion
  289.3 8.9 copy.105
  298.2 9.2 copy.85
  307.3 263.8 %all-to-all-done.1 = bf16[16,2,2048,128]{2,3,1,0:T(8,128)(2,1)} async-done(((bf16[16,2,2048,128]{2,3,1,0:T(8,128)(2,1)}), bf16[16,2,2048,128]{2,3,1,0:T(8,128)(2,1)}, u32[]{:S(2)}, u32[]{:S(2)}) %all-to-all-start.1) | async-done | bytes 16777248 | tf_op jit(solution)/shard_map/all_to_all | solution.py:98
  571.2 14.5 %concatenate.54 = bf16[2,2048,17,128]{1,3,0,2:T(8,128)(2,1)} pad(bf16[2,2048,16,128]{1,3,0,2:T(8,128)(2,1)} %bitcast.25, bf16[]{:T(256)} %constant.419.clone.1), padding=0_0x0_0x0_1x0_0 | pad | bytes 34603008 | tf_op jit(solution)/shard_map/concatenate | solution.py:101
  585.7 11.1 gather_fusion.3
  596.8 9.7 convert_reduce_fusion
  606.5 11.9 bitcast_add_fusion
  621.4 94.6 %all-reduce.12.cloned.1.call-done = f32[2048,256]{0,1:T(8,128)} async-done(((f32[2048,256]{0,1:T(8,128)}), f32[2048,256]{0,1:T(8,128)}) %all-reduce.12.cloned.1.call-update) | async-done | bytes 2097168 | tf_op jit(solution)/shard_map/psum | solution.py:161
  718.2 59.3 %all-reduce.14.cloned.1.call-done = f32[256,256]{0,1:T(8,128)} async-done(((f32[256,256]{0,1:T(8,128)}), f32[256,256]{0,1:T(8,128)}) %all-reduce.14.cloned.1.call-update) | async-done | bytes 262160 | tf_op jit(solution)/shard_map/psum | solution.py:173
  779.5 11.7 cholesky.130
  791.3 9.8 custom-call.29
  801.6 11.7 cholesky.147
  815.9 6.8 gather_fusion.4
  824.7 4.1 while.8
  828.8 19.7 %custom-call.30 = f32[2,128,128]{1,2,0:T(8,128)S(1)} custom-call(f32[2,128,128]{2,1,0:T(8,128)S(1)} %get-tuple-element.70), custom_call_target="InvertDiagBlocksLowerTriangular" | custom-call | tf_op jit(solution)/shard_map/triangular_solve/custom-call.0 | solution.py:175
  857.5 4.8 fusion.3
  863.6 61.6 %all-reduce.16.cloned.1.call-done = f32[1024,256]{0,1:T(8,128)} async-done(((f32[1024,256]{0,1:T(8,128)}), f32[1024,256]{0,1:T(8,128)}) %all-reduce.16.cloned.1.call-update) | async-done | bytes 1048592 | tf_op jit(solution)/shard_map/psum | solution.py:13
  925.1 10.8 convolution_subtract_fusion.1
  941.1 89.8 %all-reduce.18.cloned.1.call-done = f32[2048,256]{0,1:T(8,128)} async-done(((f32[2048,256]{0,1:T(8,128)}), f32[2048,256]{0,1:T(8,128)}) %all-reduce.18.cloned.1.call-update) | async-done | bytes 2097168 | tf_op jit(solution)/shard_map/psum | solution.py:161
  1032.7 59.6 %all-reduce.20.cloned.1.call-done = f32[256,256]{0,1:T(8,128)} async-done(((f32[256,256]{0,1:T(8,128)}), f32[256,256]{0,1:T(8,128)}) %all-reduce.20.cloned.1.call-update) | async-done | bytes 262160 | tf_op jit(solution)/shard_map/psum | solution.py:173
  1094.4 11.7 cholesky.164
  1106.1 9.8 custom-call.31
  1116.4 11.7 cholesky.181
  1130.8 8.8 gather_fusion.5
  1146.3 19.7 %custom-call.32 = f32[2,128,128]{1,2,0:T(8,128)S(1)} custom-call(f32[2,128,128]{2,1,0:T(8,128)S(1)} %get-tuple-element.71), custom_call_target="InvertDiagBlocksLowerTriangular" | custom-call | tf_op jit(solution)/shard_map/triangular_solve/custom-call.0 | solution.py:175
  1173.5 4.0 reshape.608
  1177.5 4.8 fusion.4
  1184.2 60.9 %all-reduce.22.cloned.1.call-done = f32[1024,256]{0,1:T(8,128)} async-done(((f32[1024,256]{0,1:T(8,128)}), f32[1024,256]{0,1:T(8,128)}) %all-reduce.22.cloned.1.call-update) | async-done | bytes 1048592 | tf_op jit(solution)/shard_map/psum | solution.py:13
  1245.1 10.9 convolution_subtract_fusion
  1260.4 5.2 copy.94
  1265.6 10.7 copy.81
  (166 shorter events, 96.9 us)
Async XLA Ops:
  99.0 77.1 %all-to-all-start = ((bf16[2,2048,768]{2,0,1:T(2,128)(2,1)}), bf16[2,2048,768]{2,0,1:T(2,128)(2,1)}, u32[]{:S(2)}, u32[]{:S(2)}) async-start(bf16[2,2048,768]{2,0,1:T(2,128)(2,1)} %copy.69), calls=%async_computation | async-start | bytes 12582912 | tf_op jit(solution)/shard_map/all_to_all | solution.py:77
  271.0 8.6 copy-start.4
  271.0 300.2 %all-to-all-start.1 = ((bf16[16,2,2048,128]{2,3,1,0:T(8,128)(2,1)}), bf16[16,2,2048,128]{2,3,1,0:T(8,128)(2,1)}, u32[]{:S(2)}, u32[]{:S(2)}) async-start(bf16[16,2,2048,128]{2,3,1,0:T(8,128)(2,1)} %fusion.9), calls=%async_computation.1 | async-start | bytes 33554432 | tf_op jit(solution)/shard_map/all_to_all | solution.py:98
  279.3 436.7 %all-reduce.12.cloned.1.call-start = ((), (), s32[]{:S(2)}) async-start(), calls=%async_computation.2 | async-start | bytes 4194304 | tf_op jit(solution)/shard_map/psum | solution.py:161
  621.3 156.2 %all-reduce.14.cloned.1.call-start = ((), (), s32[]{:S(2)}) async-start(), calls=%async_computation.3 | async-start | bytes 524288 | tf_op jit(solution)/shard_map/psum | solution.py:173
  717.7 207.5 %all-reduce.16.cloned.1.call-start = ((), (), s32[]{:S(2)}) async-start(), calls=%async_computation.4 | async-start | bytes 2097152 | tf_op jit(solution)/shard_map/psum | solution.py:13
  848.4 5.8 copy-start.3
  863.5 167.4 %all-reduce.18.cloned.1.call-start = ((), (), s32[]{:S(2)}) async-start(), calls=%async_computation.5 | async-start | bytes 4194304 | tf_op jit(solution)/shard_map/psum | solution.py:161
  936.0 3.4 copy-start
  941.1 151.2 %all-reduce.20.cloned.1.call-start = ((), (), s32[]{:S(2)}) async-start(), calls=%async_computation.6 | async-start | bytes 524288 | tf_op jit(solution)/shard_map/psum | solution.py:173
  1032.6 212.5 %all-reduce.22.cloned.1.call-start = ((), (), s32[]{:S(2)}) async-start(), calls=%async_computation.7 | async-start | bytes 2097152 | tf_op jit(solution)/shard_map/psum | solution.py:13
  1166.0 5.8 copy-start.2
  1245.1 12.7 copy-start.1
Sparse Core Ops, SparseCore 0:
  621.4 94.5 all-reduce.11
  718.4 58.9 all-reduce.13
  863.7 61.4 all-reduce.15
  941.2 89.7 all-reduce.17
  1033.2 58.9 all-reduce.19
  1183.6 61.4 all-reduce.21
